TPU v7x, 32 devices: a whole 2x2x4 slice. The times are simulated.
32 devices in a mesh: stream: 2 (over x), dp: 16 (over z, y, core).
Axes of the slice: x: 2, y: 2, z: 4, core: 2. Of those that a mesh axis runs over, the one named last changes fastest.
Arguments:
- tokens: bfloat16 [2, 16, 512, 768], P('stream', 'dp'), may hold values from -6 to 6
- boxes: int32 [2, 16, 2, 512], P('stream', 'dp'), may hold values from 0 to 1023
- rel_one: int32 [2, 16, 512, 512], P('stream', 'dp'), may hold values from 0 to 31
- rel_two: int32 [2, 16, 512, 512], P('stream', 'dp'), may hold values from 0 to 63
- vis_count: int32 [16], P('dp'), may hold values from 256 to 512, as said below
- spatial_tables: bfloat16 [2, 1024, 768], replicated, may hold values from -4.1875 to 4.1875
- proj_weights: bfloat16 [2, 2, 5, 768, 768], P('stream'), may hold values from -0.21875 to 0.21875
- out_weights: bfloat16 [2, 2, 768, 768], P('stream'), may hold values from -1.25 to 1.25
- ffn_in: bfloat16 [2, 2, 768, 3072], P('stream'), may hold values from -0.21875 to 0.21875
- ffn_out: bfloat16 [2, 2, 3072, 768], P('stream'), may hold values from -0.109375 to 0.109375
- norm_gains: float32 [2, 2, 2, 768], P('stream'), may hold values from 0.5 to 1.5
- norm_shifts: float32 [2, 2, 2, 768], P('stream'), may hold values from -1.8 to 1.8
- bias_tables: bfloat16 [2, 2, 12, 96], P('stream'), may hold values from -6 to 6
- cotangent: bfloat16 [2, 16, 512, 768], P('stream', 'dp'), may hold values from -6 to 6
Outputs:
- output: bfloat16 [2, 16, 512, 768], P('stream', 'dp')
- grad_tokens: float32 [2, 16, 512, 768], P('stream', 'dp')
- grad_spatial: float32 [2, 1024, 768], replicated
- grad_proj: float32 [2, 2, 5, 768, 768], P('stream', None, None, 'dp')
- grad_out: float32 [2, 2, 768, 768], P('stream', None, 'dp')
- grad_ffn_in: float32 [2, 2, 768, 3072], P('stream', None, 'dp')
- grad_ffn_out: float32 [2, 2, 3072, 768], P('stream', None, 'dp')
- grad_gains: float32 [2, 2, 2, 768], P('stream', None, None, 'dp')
- grad_shifts: float32 [2, 2, 2, 768], P('stream', None, None, 'dp')
- grad_tables: float32 [2, 2, 12, 96], P('stream')
Inputs may be any that keep to these rules, and one draw needn't show every extreme that they name: `vis_count`: each page has 256 or 512 visual tokens; the first page always has 512, the second 512 // 2.
All inputs are finite; a program needn't handle non-finite values.
Results may differ from a plain program's by a relative error of at most 0.035.
The roundings to bfloat16 on the way count: a program that leaves them out, or rounds other values in their place, can miss the bound.
Values sent between devices are 32-bit elements; how exact they have to be, the bound alone decides.
No kernel may reach another device: no remote copies, remote signals or barrier semaphores. Data moves between devices by JAX's collectives and lax.ppermute only.
A program may use at most 384 MiB of HBM per device.

v0:
```python
from functools import partial
import jax
import jax.numpy as jnp
from jax import lax
from jax.sharding import PartitionSpec as P

D = 768
HEADS = 12
HD = 64
NB1 = 32
NB2 = 64
LAYERS = 2
NEG_FILL = -1e30


def layer_norm(values, gain_vec, shift_vec):
    center = values - jnp.mean(values, axis=-1, keepdims=True)
    spread = jnp.mean(center * center, axis=-1, keepdims=True)
    return center * lax.rsqrt(spread + 1e-05) * gain_vec + shift_vec


def mixed_dot(formula, left, right):
    return jnp.einsum(formula, left, right, preferred_element_type=jnp.float32)


def bucket_lookup(rel_first, rel_second, bucket_table):
    first_hot = (rel_first[:, :, None] == jnp.arange(NB1, dtype=jnp.int32)[None, None, :]).astype(
        jnp.bfloat16
    )
    second_hot = (rel_second[:, :, None] == jnp.arange(NB2, dtype=jnp.int32)[None, None, :]).astype(
        jnp.bfloat16
    )
    bucket_bias = mixed_dot("qkb,hb->hqk", first_hot, bucket_table[:, :NB1]) + mixed_dot(
        "qkb,hb->hqk", second_hot, bucket_table[:, NB1:]
    )
    return (bucket_bias, first_hot, second_hot)


def page_scores(query_cat, key_cat, rel_first, rel_second, key_valid, bucket_table):
    bucket_bias, first_hot, second_hot = bucket_lookup(rel_first, rel_second, bucket_table)
    scores = mixed_dot("qhd,khd->hqk", query_cat, key_cat) * HD ** (-0.5) + bucket_bias
    scores = jnp.where(key_valid[None, None, :], scores, NEG_FILL)
    return (scores, first_hot, second_hot)


def page_forward(inputs, bucket_table):
    query_cat, key_cat, value_heads, rel_first, rel_second, key_valid = inputs
    scores, first_hot, second_hot = page_scores(
        query_cat, key_cat, rel_first, rel_second, key_valid, bucket_table
    )
    row_top = jnp.max(scores, axis=-1, keepdims=True)
    exp_scores = jnp.exp(scores - row_top)
    row_total = jnp.sum(exp_scores, axis=-1, keepdims=True)
    prob_low = (exp_scores / row_total).astype(jnp.bfloat16)
    context = mixed_dot("hqk,khd->qhd", prob_low, value_heads).astype(jnp.bfloat16)
    return (context, (row_top + jnp.log(row_total))[:, :, 0])


def page_backward(inputs, bucket_table):
    query_cat, key_cat, value_heads, rel_first, rel_second, key_valid, log_total, context_grad = (
        inputs
    )
    scores, first_hot, second_hot = page_scores(
        query_cat, key_cat, rel_first, rel_second, key_valid, bucket_table
    )
    prob_full = jnp.exp(scores - log_total[:, :, None])
    prob_low = prob_full.astype(jnp.bfloat16)
    prob_grad = mixed_dot("qhd,khd->hqk", context_grad, value_heads)
    score_grad = (
        prob_full * (prob_grad - jnp.sum(prob_full * prob_grad, axis=-1, keepdims=True))
    ).astype(jnp.bfloat16)
    score_scale = HD ** (-0.5)
    query_grad = (mixed_dot("hqk,khd->qhd", score_grad, key_cat) * score_scale).astype(jnp.bfloat16)
    key_grad = (mixed_dot("hqk,qhd->khd", score_grad, query_cat) * score_scale).astype(jnp.bfloat16)
    value_grad = mixed_dot("hqk,qhd->khd", prob_low, context_grad).astype(jnp.bfloat16)
    table_grad = jnp.concatenate(
        [
            mixed_dot("hqk,qkb->hb", score_grad, first_hot),
            mixed_dot("hqk,qkb->hb", score_grad, second_hot),
        ],
        axis=1,
    )
    return (query_grad, key_grad, value_grad, table_grad)


def head_layout(token_proj, spatial_proj, page_count):
    length = token_proj.shape[1] // page_count

    def to_heads(values):
        return values.reshape(page_count, length, HEADS, HD)

    query_cat = jnp.concatenate([to_heads(token_proj[0]), to_heads(spatial_proj[0])], axis=-1)
    key_cat = jnp.concatenate([to_heads(token_proj[1]), to_heads(spatial_proj[1])], axis=-1)
    return (query_cat, key_cat, to_heads(token_proj[2]))


def layer_forward(hidden_in, spatial, weights, layout):
    projections, out_proj, w_in, w_out, gains, shifts, bucket_table = weights
    rel_first, rel_second, key_valid, rowmask = layout
    page_count = rel_first.shape[0]
    row_count = hidden_in.shape[0]
    rounded = hidden_in.astype(jnp.bfloat16)
    token_proj = mixed_dot("rd,jde->jre", rounded, projections[:3]).astype(jnp.bfloat16)
    spatial_proj = mixed_dot("rd,jde->jre", spatial, projections[3:]).astype(jnp.bfloat16)
    query_cat, key_cat, value_heads = head_layout(token_proj, spatial_proj, page_count)
    context, log_total = lax.map(
        partial(page_forward, bucket_table=bucket_table),
        (query_cat, key_cat, value_heads, rel_first, rel_second, key_valid),
    )
    context = context.reshape(row_count, D)
    attn_out = jnp.dot(context, out_proj, preferred_element_type=jnp.float32) * rowmask
    mixed = lax.psum(attn_out, "stream")
    pre_attn = hidden_in + mixed
    normed = layer_norm(pre_attn, gains[0], shifts[0])
    normed_low = normed.astype(jnp.bfloat16)
    inner_pre = jnp.dot(normed_low, w_in, preferred_element_type=jnp.float32)
    activated = jax.nn.gelu(inner_pre, approximate=False).astype(jnp.bfloat16)
    branch = jnp.dot(activated, w_out, preferred_element_type=jnp.float32)
    result = layer_norm(normed + branch, gains[1], shifts[1])
    kept_state = (
        rounded,
        token_proj,
        spatial_proj,
        context,
        log_total,
        pre_attn,
        normed,
        normed_low,
        inner_pre,
        activated,
        branch,
    )
    return (result, kept_state)


def gelu_exact(values):
    return jax.nn.gelu(values, approximate=False)


def layer_backward(result_grad, spatial, weights, layout, kept_state):
    projections, out_proj, w_in, w_out, gains, shifts, bucket_table = weights
    rel_first, rel_second, key_valid, rowmask = layout
    (
        rounded,
        token_proj,
        spatial_proj,
        context,
        log_total,
        pre_attn,
        normed,
        normed_low,
        inner_pre,
        activated,
        branch,
    ) = kept_state
    page_count = rel_first.shape[0]
    row_count = rounded.shape[0]
    length = row_count // page_count
    unused, norm_pull = jax.vjp(layer_norm, normed + branch, gains[1], shifts[1])
    sum_grad, gain_two, shift_two = norm_pull(result_grad)
    branch_low = sum_grad.astype(jnp.bfloat16)
    w_out_grad = mixed_dot("rf,rd->fd", activated, branch_low)
    act_grad = mixed_dot("rd,fd->rf", branch_low, w_out)
    unused, gelu_pull = jax.vjp(gelu_exact, inner_pre)
    inner_low = gelu_pull(act_grad)[0].astype(jnp.bfloat16)
    w_in_grad = mixed_dot("rd,rf->df", normed_low, inner_low)
    normed_grad = sum_grad + mixed_dot("rf,df->rd", inner_low, w_in)
    unused, first_pull = jax.vjp(layer_norm, pre_attn, gains[0], shifts[0])
    pre_grad, gain_one, shift_one = first_pull(normed_grad)
    mixed_grad = lax.psum(pre_grad, "stream")
    attn_low = (mixed_grad * rowmask).astype(jnp.bfloat16)
    out_grad = mixed_dot("rd,re->de", context, attn_low)
    context_grad = mixed_dot("re,de->rd", attn_low, out_proj).astype(jnp.bfloat16)
    query_cat, key_cat, value_heads = head_layout(token_proj, spatial_proj, page_count)
    query_grad, key_grad, value_grad, table_grads = lax.map(
        partial(page_backward, bucket_table=bucket_table),
        (
            query_cat,
            key_cat,
            value_heads,
            rel_first,
            rel_second,
            key_valid,
            log_total,
            context_grad.reshape(page_count, length, HEADS, HD),
        ),
    )
    token_grads = jnp.stack(
        [
            query_grad[..., :HD].reshape(row_count, D),
            key_grad[..., :HD].reshape(row_count, D),
            value_grad.reshape(row_count, D),
        ]
    )
    spatial_grads = jnp.stack(
        [query_grad[..., HD:].reshape(row_count, D), key_grad[..., HD:].reshape(row_count, D)]
    )
    proj_grad = jnp.concatenate(
        [
            mixed_dot("rd,jre->jde", rounded, token_grads),
            mixed_dot("rd,jre->jde", spatial, spatial_grads),
        ],
        axis=0,
    )
    input_grad = pre_grad + mixed_dot("jre,jde->rd", token_grads, projections[:3])
    spatial_part = mixed_dot("jre,jde->rd", spatial_grads, projections[3:])
    weight_grads = (
        proj_grad,
        out_grad,
        w_in_grad,
        w_out_grad,
        jnp.stack([gain_one, gain_two]),
        jnp.stack([shift_one, shift_two]),
    )
    return (input_grad, spatial_part, weight_grads, jnp.sum(table_grads, axis=0))


def local(
    tokens,
    boxes,
    rel_one,
    rel_two,
    vis_count,
    spatial_tables,
    proj_weights,
    out_weights,
    ffn_in,
    ffn_out,
    norm_gains,
    norm_shifts,
    bias_tables,
    cotangent,
):
    page_count = tokens.shape[1]
    length = tokens.shape[2]
    row_count = page_count * length
    stream_at = lax.axis_index("stream")
    counts = jnp.where(stream_at == 0, length, vis_count)
    key_valid = jnp.arange(length, dtype=jnp.int32)[None, :] < counts[:, None]
    rowmask = key_valid.reshape(row_count, 1).astype(jnp.float32)
    layout = (rel_one[0], rel_two[0], key_valid, rowmask)
    bin_ids = jnp.arange(spatial_tables.shape[1], dtype=jnp.int32)
    hot_x = (boxes[0, :, 0].reshape(row_count, 1) == bin_ids[None, :]).astype(jnp.bfloat16)
    hot_y = (boxes[0, :, 1].reshape(row_count, 1) == bin_ids[None, :]).astype(jnp.bfloat16)
    spatial = (
        jnp.dot(hot_x, spatial_tables[0], preferred_element_type=jnp.float32)
        + jnp.dot(hot_y, spatial_tables[1], preferred_element_type=jnp.float32)
    ).astype(jnp.bfloat16)

    def layer_weights(layer_at):
        return (
            proj_weights[0, layer_at],
            out_weights[0, layer_at],
            ffn_in[0, layer_at],
            ffn_out[0, layer_at],
            norm_gains[0, layer_at],
            norm_shifts[0, layer_at],
            bias_tables[0, layer_at],
        )

    hidden = tokens[0].reshape(row_count, D).astype(jnp.float32)
    inputs_kept = []
    states_kept = []
    for layer_at in range(LAYERS):
        inputs_kept.append(hidden)
        hidden, kept_state = layer_forward(hidden, spatial, layer_weights(layer_at), layout)
        states_kept.append(kept_state)
    output = (hidden * rowmask).astype(jnp.bfloat16).reshape(1, page_count, length, D)
    result_grad = cotangent[0].reshape(row_count, D).astype(jnp.float32) * rowmask
    spatial_grad = jnp.zeros((row_count, D), jnp.float32)
    layer_grads = []
    table_grads = []
    for layer_at in reversed(range(LAYERS)):
        kept_state = states_kept[layer_at]
        result_grad, spatial_part, weight_grads, table_part = layer_backward(
            result_grad, spatial, layer_weights(layer_at), layout, kept_state
        )
        spatial_grad = spatial_grad + spatial_part
        layer_grads.insert(0, weight_grads)
        table_grads.insert(0, table_part)
    stacked = tuple((jnp.stack(members) for members in zip(*layer_grads)))
    stacked = (
        lax.psum_scatter(stacked[0], "dp", scatter_dimension=2, tiled=True),
        lax.psum_scatter(stacked[1], "dp", scatter_dimension=1, tiled=True),
        lax.psum_scatter(stacked[2], "dp", scatter_dimension=1, tiled=True),
        lax.psum_scatter(stacked[3], "dp", scatter_dimension=1, tiled=True),
        lax.psum_scatter(stacked[4], "dp", scatter_dimension=2, tiled=True),
        lax.psum_scatter(stacked[5], "dp", scatter_dimension=2, tiled=True),
    )
    spatial_low = spatial_grad.astype(jnp.bfloat16)
    table_x = mixed_dot("rb,rd->bd", hot_x, spatial_low)
    table_y = mixed_dot("rb,rd->bd", hot_y, spatial_low)
    own_slot = (jnp.arange(2, dtype=jnp.int32) == stream_at).astype(jnp.float32)
    bucket_all = own_slot[:, None, None, None] * jnp.stack(table_grads)[None]
    shared, buckets = lax.psum((jnp.stack([table_x, table_y]), bucket_all), ("stream", "dp"))
    bucket_own = lax.dynamic_slice_in_dim(buckets, stream_at, 1, 0)
    return (
        output,
        result_grad.reshape(1, page_count, length, D),
        shared,
        stacked[0][None],
        stacked[1][None],
        stacked[2][None],
        stacked[3][None],
        stacked[4][None],
        stacked[5][None],
        bucket_own,
    )


def solution(mesh):
    placed = (
        P("stream", "dp", None, None),
        P("stream", "dp", None, None),
        P("stream", "dp", None, None),
        P("stream", "dp", None, None),
        P("dp"),
        P(),
        P("stream", None, None, None, None),
        P("stream", None, None, None),
        P("stream", None, None, None),
        P("stream", None, None, None),
        P("stream", None, None, None),
        P("stream", None, None, None),
        P("stream", None, None, None),
        P("stream", "dp", None, None),
    )
    return jax.shard_map(
        local,
        mesh=mesh,
        in_specs=placed,
        out_specs=(
            P("stream", "dp", None, None),
            P("stream", "dp", None, None),
            P(),
            P("stream", None, None, "dp", None),
            P("stream", None, "dp", None),
            P("stream", None, "dp", None),
            P("stream", None, "dp", None),
            P("stream", None, None, "dp"),
            P("stream", None, None, "dp"),
            P("stream", None, None, None),
        ),
        check_vma=False,
    )
```

profile of v0, /device:TPU:0, one launch (start us, length us, event | category | flops | bytes accessed | tf_op | source)
XLA Modules:
  0.0 1694.1 jit_solution(16295816301324897043)
XLA Ops:
  7.2 4.3 convert_bitcast_fusion.1
  15.2 14.9 fusion.3
  30.2 8.5 fusion.11
  41.0 3.3 fusion.130
  60.7 31.0 %fusion.242 = (f32[12,512]{1,0:T(8,128)S(1)}, f32[12,512,512]{1,2,0:T(8,128)}) fusion(f32[512,512,12]{0,2,1:T(8,128)} %fusion.3, f32[512,512,12]{0,2,1:T(8,128)} %fusion.11, bf16[1,512,12,64]{3,1,2,0:T(8,128)(2,1)} %copy.153, bf16[1,512,12,64]{3,1,2,0:T(8,128)(2,1)} %copy.152, bf16[1,512,12,64]{3,1,2,0:T(8,128)(2,1)} %copy.150, ...), kind=kOutput, calls=%fused_computation.338 | convolution fusion | flops 827320320 | bytes 40919552 | tf_op jit(solution)/shard_map/while/body/eval_jaxpr/qhd,khd->hqk/dot_general | solution.py:23
  91.8 6.6 fusion.18
  105.4 3.1 fusion.127
  118.5 8.6 fusion.10
  127.1 14.4 fusion.2
  141.5 18.1 %all-reduce.8.cloned.1.call-done = f32[512,768]{1,0:T(8,128)} async-done(((f32[512,768]{1,0:T(8,128)}), f32[512,768]{1,0:T(8,128)}) %all-reduce.8.cloned.1.call-update) | async-done | bytes 1572880 | tf_op jit(solution)/shard_map/psum | solution.py:112
  162.6 20.2 %multiply_convert_fusion.3 = (bf16[512,3072]{1,0:T(8,128)(2,1)S(1)}, f32[512,3072]{1,0:T(8,128)}, f32[512,3072]{1,0:T(8,128)}) fusion(bf16[1,2,768,3072]{3,2,1,0:T(8,128)(2,1)} %param.22, f32[512,768]{1,0:T(8,128)S(1)} %get-tuple-element.219, f32[768]{0:T(1024)S(1)} %get-tuple-element.202, f32[768]{0:T(1024)S(1)} %get-tuple-element.265, ...), kind=kOutput, calls=%fused_computation.71 | convolution fusion | flops 2520121344 | bytes 22030336 | tf_op jit(solution)/shard_map/dot_general | solution.py:116
  182.9 2.7 fusion.243
  186.7 4.1 convert_bitcast_fusion
  201.6 30.3 %fusion.244 = (f32[12,512]{1,0:T(8,128)S(1)}, f32[12,512,512]{1,2,0:T(8,128)}) fusion(f32[512,512,12]{0,2,1:T(8,128)} %fusion.2, f32[512,512,12]{0,2,1:T(8,128)} %fusion.10, bf16[1,512,12,64]{3,1,2,0:T(8,128)(2,1)S(1)} %copy-done.12, bf16[1,512,12,64]{3,1,2,0:T(8,128)(2,1)} %copy.169, bf16[1,512,12,64]{3,1,2,0:T(8,128)(2,1)S(1)} %copy-done.13, ...), kind=kOutput, calls=%fused_computation.340 | convolution fusion | flops 827320320 | bytes 40919552 | tf_op jit(solution)/shard_map/while/body/eval_jaxpr/qhd,khd->hqk/dot_general | solution.py:23
  231.9 6.6 fusion.19
  240.0 3.8 fusion.161
  246.8 51.6 %all-reduce.10.cloned.1.call-done = f32[512,768]{1,0:T(8,128)} async-done(((f32[512,768]{1,0:T(8,128)}), f32[512,768]{1,0:T(8,128)}) %all-reduce.10.cloned.1.call-update) | async-done | bytes 1572880 | tf_op jit(solution)/shard_map/psum | solution.py:112
  301.3 20.1 %multiply_convert_fusion.2 = (bf16[512,3072]{1,0:T(8,128)(2,1)S(1)}, f32[512,3072]{1,0:T(8,128)}, f32[512,3072]{1,0:T(8,128)}) fusion(bf16[1,2,768,3072]{3,2,1,0:T(8,128)(2,1)} %param.22, f32[512,768]{1,0:T(8,128)S(1)} %get-tuple-element.215, f32[768]{0:T(1024)S(1)} %get-tuple-element.203, f32[768]{0:T(1024)S(1)} %get-tuple-element.264, ...), kind=kOutput, calls=%fused_computation.58 | convolution fusion | flops 2520121344 | bytes 22030336 | tf_op jit(solution)/shard_map/dot_general | solution.py:116
  321.5 2.8 fusion.245
  327.1 8.8 add_convert_fusion.1
  335.9 6.6 multiply_reduce_fusion.2
  344.8 51.5 %all-reduce.12.cloned.1.call-done = f32[512,768]{1,0:T(8,128)} async-done(((f32[512,768]{1,0:T(8,128)}), f32[512,768]{1,0:T(8,128)}) %all-reduce.12.cloned.1.call-update) | async-done | bytes 1572880 | tf_op jit(solution)/shard_map/psum | solution.py:170
  396.3 3.5 convolution_convert_fusion.1
  402.1 7.9 fusion.155
  410.0 9.4 multiply_reduce_fusion.1
  419.4 7.0 multiply_convert_fusion.1
  426.4 3.4 fusion.136
  429.9 2.9 fusion.135
  443.8 5.2 multiply_reduce_fusion.3
  449.8 10.1 add_convert_fusion
  460.0 5.0 multiply_reduce_fusion.4
  475.3 5.4 convolution_bitcast_fusion.6
  480.7 5.1 convolution_bitcast_fusion.4
  485.8 10.0 maximum_bitcast_fusion.1
  497.7 21.0 %all-reduce.14.cloned.1.call-done = f32[512,768]{1,0:T(8,128)} async-done(((f32[512,768]{1,0:T(8,128)}), f32[512,768]{1,0:T(8,128)}) %all-reduce.14.cloned.1.call-update) | async-done | bytes 1572880 | tf_op jit(solution)/shard_map/psum | solution.py:170
  521.6 7.7 fusion.158
  529.3 9.2 multiply_reduce_fusion
  538.5 7.2 multiply_convert_fusion
  545.8 3.4 fusion.138
  566.7 4.9 convolution_bitcast_fusion.7
  571.6 4.9 convolution_bitcast_fusion.5
  576.5 10.1 maximum_bitcast_fusion
  586.6 16.6 pad_maximum_fusion
  603.2 35.0 %copy.204 = f32[2,5,768,768]{3,0,1,2:T(2,128)} copy(f32[2,5,768,768]{2,3,1,0:T(8,128)} %pad_maximum_fusion) | data formatting | bytes 47185920 | tf_op jit(solution)/shard_map/stack | solution.py:281
  639.6 3.2 fusion.86
  642.8 3.3 fusion.121
  648.4 3.1 pad_maximum_fusion.3
  660.1 5.0 convolution_bitcast_fusion.2
  665.1 2.9 convolution_bitcast_fusion.3
  668.0 7.0 pad_maximum_fusion.1
  676.4 4.9 convolution_bitcast_fusion
  684.1 7.0 pad_maximum_fusion.2
  693.0 10.1 fusion.177
  703.1 14.1 fusion.183
  720.3 10.6 fusion.174
  730.9 14.0 fusion.180
  745.1 40.8 %psum.47 = f32[2,2,12,96]{3,1,2,0:T(2,128)S(1)} all-reduce(f32[2,2,12,96]{3,1,2,0:T(2,128)S(1)} %broadcast_multiply_fusion), channel_id=1, replica_groups=mesh['stream'=2,'dp'=16] {'stream','dp'}, use_global_device_ids=true, to_apply=%region_41.42 | all-reduce | flops 4608 | bytes 36864 | tf_op jit(solution)/shard_map/psum | solution.py:295
  786.5 5.9 fusion.122
  792.4 249.3 %all-reduce.18.cloned.1.call-done = f32[2,5,768,768]{3,0,1,2:T(2,128)} async-done(((f32[2,5,768,768]{3,0,1,2:T(2,128)}), f32[2,5,768,768]{3,0,1,2:T(2,128)}) %all-reduce.18.cloned.1.call-update) | async-done | bytes 23592976
  1044.9 159.0 %all-reduce.16.cloned.1.call-done = f32[2,1024,768]{2,1,0:T(8,128)} async-done(((f32[2,1024,768]{2,1,0:T(8,128)}), f32[2,1024,768]{2,1,0:T(8,128)}) %all-reduce.16.cloned.1.call-update) | async-done | bytes 6291472 | tf_op jit(solution)/shard_map/psum | solution.py:295
  1203.9 80.3 %reduce-scatter.10.cloned.1.call-done = f32[2,48,768]{2,1,0:T(8,128)} async-done(((f32[2,768,768]{2,1,0:T(8,128)}), f32[2,48,768]{2,1,0:T(8,128)}) %reduce-scatter.10.cloned.1.call-update) | async-done | bytes 294928 | tf_op jit(solution)/shard_map/reduce_scatter | solution.py:284
  1284.2 198.6 %reduce-scatter.12.cloned.1.call-done = f32[2,48,3072]{2,1,0:T(8,128)} async-done(((f32[2,768,3072]{2,1,0:T(8,128)}), f32[2,48,3072]{2,1,0:T(8,128)}) %reduce-scatter.12.cloned.1.call-update) | async-done | bytes 1179664 | tf_op jit(solution)/shard_map/reduce_scatter | solution.py:285
  1482.8 198.8 %reduce-scatter.14.cloned.1.call-done = f32[2,192,768]{2,1,0:T(8,128)} async-done(((f32[2,3072,768]{2,1,0:T(8,128)}), f32[2,192,768]{2,1,0:T(8,128)}) %reduce-scatter.14.cloned.1.call-update) | async-done | bytes 1179664 | tf_op jit(solution)/shard_map/reduce_scatter | solution.py:286
  1681.5 5.9 copy.280
  (381 shorter events, 136.6 us)
Async XLA Ops:
  7.2 152.5 %all-reduce.8.cloned.1.call-start = ((), (), s32[]{:S(2)}) async-start(), calls=%async_computation.5 | async-start | bytes 3145728 | tf_op jit(solution)/shard_map/psum | solution.py:112
  12.9 85.5 %copy-start.25 = (bf16[1,512,768]{1,2,0:T(8,128)(2,1)}, bf16[1,512,768]{1,2,0:T(8,128)(2,1)S(1)}, u32[]{:S(2)}) copy-start(bf16[1,512,768]{1,2,0:T(8,128)(2,1)S(1)} %get-tuple-element.225) | copy-start | bytes 2359300
  13.3 113.9 %copy-start.6 = (s32[512,512]{0,1:T(8,128)}, s32[512,512]{0,1:T(8,128)S(1)}, u32[]{:S(2)}) copy-start(s32[512,512]{0,1:T(8,128)S(1)} %copy.157) | copy-start | bytes 3145732
  15.2 103.3 %copy-start.4 = (s32[512,512]{0,1:T(8,128)}, s32[512,512]{0,1:T(8,128)S(1)}, u32[]{:S(2)}) copy-start(s32[512,512]{0,1:T(8,128)S(1)} %copy.154) | copy-start | bytes 3145732
  30.2 8.5 copy-start.86
  30.2 8.6 copy-start.93
  91.8 8.2 copy-start
  105.3 193.1 %all-reduce.10.cloned.1.call-start = ((), (), s32[]{:S(2)}) async-start(), calls=%async_computation.6 | async-start | bytes 3145728 | tf_op jit(solution)/shard_map/psum | solution.py:112
  118.5 64.3 %copy-start.71 = (f32[768]{0:T(1024)}, f32[768]{0:T(1024)S(1)}, u32[]{:S(2)}) copy-start(f32[768]{0:T(1024)S(1)} %get-tuple-element.265) | copy-start | bytes 9220
  118.5 64.3 %copy-start.82 = (f32[768]{0:T(1024)}, f32[768]{0:T(1024)S(1)}, u32[]{:S(2)}) copy-start(f32[768]{0:T(1024)S(1)} %get-tuple-element.202) | copy-start | bytes 9220
  118.5 202.9 %copy-start.84 = (f32[768]{0:T(1024)}, f32[768]{0:T(1024)S(1)}, u32[]{:S(2)}) copy-start(f32[768]{0:T(1024)S(1)} %get-tuple-element.203) | copy-start | bytes 9220
  118.5 224.1 %copy-start.73 = (f32[768]{0:T(1024)}, f32[768]{0:T(1024)S(1)}, u32[]{:S(2)}) copy-start(f32[768]{0:T(1024)S(1)} %get-tuple-element.264) | copy-start | bytes 9220
  127.1 32.5 %copy-start.44 = (bf16[1,1,512,768]{3,2,1,0:T(8,128)(2,1)S(1)}, bf16[1,1,512,768]{3,2,1,0:T(8,128)(2,1)}, u32[]{:S(2)}) copy-start(bf16[1,1,512,768]{3,2,1,0:T(8,128)(2,1)} %param.14) | copy-start | bytes 2359300
  159.7 23.2 %slice-start.6 = ((s8[9437184]{0:T(1024)(128)(4,1)}), s8[4194304]{0:T(1024)(128)(4,1)S(1)}, s32[]{:S(2)}) async-start(s8[9437184]{0:T(1024)(128)(4,1)} %bitcast.390), calls=%async_computation.22 | async-start | bytes 8388608
  161.5 21.3 %copy-start.16 = (f32[512,768]{1,0:T(8,128)}, f32[512,768]{1,0:T(8,128)S(1)}, u32[]{:S(2)}) copy-start(f32[512,768]{1,0:T(8,128)S(1)} %get-tuple-element.219) | copy-start | bytes 4718596
  161.5 21.3 %copy-start.63 = (f32[512]{0:T(512)}, f32[512]{0:T(512)S(1)}, u32[]{:S(2)}) copy-start(f32[512]{0:T(512)S(1)} %broadcast_multiply_fusion.4) | copy-start | bytes 6148
  162.6 20.2 %copy-start.78 = (f32[512]{0:T(512)}, f32[512]{0:T(512)S(1)}, u32[]{:S(2)}) copy-start(f32[512]{0:T(512)S(1)} %fusion.198) | copy-start | bytes 6148
  162.6 20.3 %slice-start.7 = ((s8[9437184]{0:T(1024)(128)(4,1)}), s8[4194304]{0:T(1024)(128)(4,1)S(1)}, s32[]{:S(2)}) async-start(s8[9437184]{0:T(1024)(128)(4,1)} %bitcast.390), calls=%async_computation.23 | async-start | bytes 8388608
  162.6 20.3 %slice-start.8 = ((s8[9437184]{0:T(1024)(128)(4,1)}), s8[1048576]{0:T(1024)(128)(4,1)S(1)}, s32[]{:S(2)}) async-start(s8[9437184]{0:T(1024)(128)(4,1)} %bitcast.390), calls=%async_computation.24 | async-start | bytes 2097152
  194.2 7.4 copy-start.12
  194.2 7.4 copy-start.13
  231.9 8.2 copy-start.1
  246.7 149.6 %all-reduce.12.cloned.1.call-start = ((), (), s32[]{:S(2)}) async-start(), calls=%async_computation.7 | async-start | bytes 3145728 | tf_op jit(solution)/shard_map/psum | solution.py:170
  298.4 23.0 %slice-start.9 = ((s8[9437184]{0:T(1024)(128)(4,1)}), s8[4194304]{0:T(1024)(128)(4,1)S(1)}, s32[]{:S(2)}) async-start(s8[9437184]{0:T(1024)(128)(4,1)} %bitcast.392), calls=%async_computation.25 | async-start | bytes 8388608
  300.9 41.7 %copy-start.18 = (f32[512,768]{1,0:T(8,128)}, f32[512,768]{1,0:T(8,128)S(1)}, u32[]{:S(2)}) copy-start(f32[512,768]{1,0:T(8,128)S(1)} %get-tuple-element.215) | copy-start | bytes 4718596
  300.9 41.7 %copy-start.65 = (f32[512]{0:T(512)}, f32[512]{0:T(512)S(1)}, u32[]{:S(2)}) copy-start(f32[512]{0:T(512)S(1)} %broadcast_multiply_fusion.2) | copy-start | bytes 6148
  301.2 41.4 %copy-start.80 = (f32[512]{0:T(512)}, f32[512]{0:T(512)S(1)}, u32[]{:S(2)}) copy-start(f32[512]{0:T(512)S(1)} %fusion.200) | copy-start | bytes 6148
  301.3 20.2 %slice-start.10 = ((s8[9437184]{0:T(1024)(128)(4,1)}), s8[4194304]{0:T(1024)(128)(4,1)S(1)}, s32[]{:S(2)}) async-start(s8[9437184]{0:T(1024)(128)(4,1)} %bitcast.392), calls=%async_computation.26 | async-start | bytes 8388608
  301.3 20.2 %slice-start.11 = ((s8[9437184]{0:T(1024)(128)(4,1)}), s8[1048576]{0:T(1024)(128)(4,1)S(1)}, s32[]{:S(2)}) async-start(s8[9437184]{0:T(1024)(128)(4,1)} %bitcast.392), calls=%async_computation.27 | async-start | bytes 2097152
  327.1 8.8 copy-start.37
  327.1 8.8 copy-start.87
  344.7 174.0 %all-reduce.14.cloned.1.call-start = ((), (), s32[]{:S(2)}) async-start(), calls=%async_computation.8 | async-start | bytes 3145728 | tf_op jit(solution)/shard_map/psum | solution.py:170
  402.1 7.9 copy-start.22
  402.1 7.9 copy-start.27
  402.1 17.3 %slice-start.3 = ((s8[12582912]{0:T(1024)(128)(4,1)}), s8[4194304]{0:T(1024)(128)(4,1)S(1)}, s32[]{:S(2)}) async-start(s8[12582912]{0:T(1024)(128)(4,1)} %bitcast.346), calls=%async_computation.19 | async-start | bytes 8388608
  402.1 17.3 %slice-start.4 = ((s8[12582912]{0:T(1024)(128)(4,1)}), s8[4194304]{0:T(1024)(128)(4,1)S(1)}, s32[]{:S(2)}) async-start(s8[12582912]{0:T(1024)(128)(4,1)} %bitcast.346), calls=%async_computation.20 | async-start | bytes 8388608
  410.0 9.4 slice-start.5
  436.3 7.5 copy-start.21
  436.4 7.5 copy-start.23
  443.8 16.1 slice-start.12
  443.8 16.1 slice-start.13
  449.7 10.2 copy-start.40
  449.7 10.2 copy-start.17
  449.8 10.2 copy-start.64
  449.8 10.2 copy-start.72
  449.8 10.2 copy-start.79
  449.8 10.2 slice-start.14
  467.0 250.2 %reduce-scatter.16.cloned.1.call-start = ((), (), s32[]{:S(2)}) async-start(), calls=%async_computation.13 | async-start | bytes 417792
  495.9 222.9 %reduce-scatter.18.cloned.1.call-start = ((), (), s32[]{:S(2)}) async-start(), calls=%async_computation.14 | async-start | bytes 417792
  497.7 544.1 %all-reduce.18.cloned.1.call-start = ((), (), s32[]{:S(2)}) async-start(), calls=%async_computation.15 | async-start | bytes 47185920
  521.6 7.7 copy-start.26
  521.6 16.9 slice-start
  521.6 16.8 slice-start.1
  529.3 9.2 slice-start.2
  538.5 7.3 copy-start.10
  538.5 7.3 copy-start.11
  564.0 7.6 copy-start.33
  638.2 565.7 %all-reduce.16.cloned.1.call-start = ((), (), s32[]{:S(2)}) async-start(), calls=%async_computation.9 | async-start | bytes 12582912 | tf_op jit(solution)/shard_map/psum | solution.py:295
  651.6 632.6 %reduce-scatter.10.cloned.1.call-start = ((), (), s32[]{:S(2)}) async-start(), calls=%async_computation.10 | async-start | bytes 5013504 | tf_op jit(solution)/shard_map/reduce_scatter | solution.py:284
  658.6 824.1 %reduce-scatter.12.cloned.1.call-start = ((), (), s32[]{:S(2)}) async-start(), calls=%async_computation.11 | async-start | bytes 20054016 | tf_op jit(solution)/shard_map/reduce_scatter | solution.py:285
  675.0 1006.5 %reduce-scatter.14.cloned.1.call-start = ((), (), s32[]{:S(2)}) async-start(), calls=%async_computation.12 | async-start | bytes 20054016 | tf_op jit(solution)/shard_map/reduce_scatter | solution.py:286
  692.9 10.2 copy-start.7
  730.9 55.6 %copy-start.47 = (bf16[1,512,768]{2,1,0:T(8,128)(2,1)S(1)}, bf16[1,512,768]{2,1,0:T(8,128)(2,1)}, u32[]{:S(2)}) copy-start(bf16[1,512,768]{2,1,0:T(8,128)(2,1)} %copy.194) | copy-start | bytes 2359300
  730.9 55.6 %copy-start.49 = (bf16[1,512,768]{2,1,0:T(8,128)(2,1)S(1)}, bf16[1,512,768]{2,1,0:T(8,128)(2,1)}, u32[]{:S(2)}) copy-start(bf16[1,512,768]{2,1,0:T(8,128)(2,1)} %copy.193) | copy-start | bytes 2359300
  (64 other events, 214.0 us)
Sparse Core Ops, SparseCore 0:
  105.4 54.1 all-reduce.7
  246.8 51.4 all-reduce.9
  344.8 51.4 all-reduce.11
  467.2 51.5 all-reduce.13
  522.0 55.6 reduce-scatter.15
  581.5 54.5 reduce-scatter.17
  639.9 401.8 all-reduce.17
  1048.0 155.9 all-reduce.15
  1208.8 75.2 reduce-scatter.9
  1288.7 194.0 reduce-scatter.11
  1487.5 194.0 reduce-scatter.13
where the time goes:
time: 1700 us; the launch traced here: 1690 us
  waiting for transfers between devices  1030 us (61%)
  matrix products  371 us (22%)
  local copies, waits for them, and re-layouts  140 us (8%)
  other arithmetic  96.8 us (6%)
  blocking collectives  40.8 us (2%)
  between operations  17 us (1%)
    dot_general x46, matrix products, mixed_dot(): return jnp.einsum(formula, left, right, preferred_element_type=jnp.float32)  319 us
    unnamed x14, waiting for transfers between devices  250 us
    reduce_scatter x1, waiting for transfers between devices, local(): lax.psum_scatter(stacked[3], 'dp', scatter_dimension=1, tiled=True)  199 us
    reduce_scatter x1, waiting for transfers between devices, local(): lax.psum_scatter(stacked[2], 'dp', scatter_dimension=1, tiled=True)  199 us
    psum x1, waiting for transfers between devices, local(): lax.psum((jnp.stack([table_x, table_y]), bucket_all), ('stream', 'dp'))  159 us
    reduce_scatter x1, waiting for transfers between devices, local(): lax.psum_scatter(stacked[1], 'dp', scatter_dimension=1, tiled=True)  80.3 us
    psum x2, waiting for transfers between devices, layer_backward(): mixed_grad = lax.psum(pre_grad, 'stream')  72.4 us
    psum x2, waiting for transfers between devices, layer_forward(): mixed = lax.psum(attn_out, 'stream')  69.7 us
  transfers between devices with their start and end apart: 11, of which 9 were waited for; matrix products, arithmetic and copies ran while one was open for 17% of the time, Pallas kernels for 0%

commit v1 on v0

--- a/solution.py
+++ b/solution.py
@@ -292,7 +292,9 @@
     table_y = mixed_dot("rb,rd->bd", hot_y, spatial_low)
     own_slot = (jnp.arange(2, dtype=jnp.int32) == stream_at).astype(jnp.float32)
     bucket_all = own_slot[:, None, None, None] * jnp.stack(table_grads)[None]
-    shared, buckets = lax.psum((jnp.stack([table_x, table_y]), bucket_all), ("stream", "dp"))
+    shared, buckets = lax.psum(
+        lax.psum((jnp.stack([table_x, table_y]), bucket_all), "dp"), "stream"
+    )
     bucket_own = lax.dynamic_slice_in_dim(buckets, stream_at, 1, 0)
     return (
         output,

time: 1700 us -> 1930 us (1.14)
  waiting for transfers between devices: 1030 us -> 1230 us
  blocking collectives: 40.8 us -> 67.2 us
    psum x1 -> x2, waiting for transfers between devices: 159 us -> 632 us  [the longest x1 500 us: local(): lax.psum((jnp.stack([table_x, table_y]), bucket_all), 'dp')]
    unnamed x14 -> x13, waiting for transfers between devices: 250 us -> 58.7 us
    reduce_scatter x1, waiting for transfers between devices: 80.3 us -> 0.01 us  [local(): lax.psum_scatter(stacked[1], 'dp', scatter_dimension=1, tiled=True)]
    psum x1 -> x2, blocking collectives: 40.8 us -> 67.2 us  [the longest x1 58.5 us: local(): lax.psum((jnp.stack([table_x, table_y]), bucket_all), 'dp')]
  transfers between devices with their start and end apart: 11 -> 11, of which waited for: 9 -> 10; matrix products, arithmetic and copies ran while one was open for 17% -> 9% of each run, Pallas kernels for 0% -> 0%
where the time goes in v1:
time: 1930 us
  waiting for transfers between devices  1230 us (64%)
  matrix products  379 us (20%)
  local copies, waits for them, and re-layouts  130 us (7%)
  other arithmetic  100 us (5%)
  blocking collectives  67.2 us (3%)
    psum x1, waiting for transfers between devices, local(): lax.psum((jnp.stack([table_x, table_y]), bucket_all), 'dp')  500 us
    dot_general x46, matrix products, mixed_dot(): return jnp.einsum(formula, left, right, preferred_element_type=jnp.float32)  326 us
    reduce_scatter x1, waiting for transfers between devices, local(): lax.psum_scatter(stacked[3], 'dp', scatter_dimension=1, tiled=True)  200 us
    reduce_scatter x1, waiting for transfers between devices, local(): lax.psum_scatter(stacked[2], 'dp', scatter_dimension=1, tiled=True)  199 us
    psum x1, waiting for transfers between devices, local(): lax.psum(lax.psum((jnp.stack([table_x, table_y]), bucket_all), 'dp'), 'st...  132 us
    psum x2, waiting for transfers between devices, layer_backward(): mixed_grad = lax.psum(pre_grad, 'stream')  73.4 us
    psum x2, waiting for transfers between devices, layer_forward(): mixed = lax.psum(attn_out, 'stream')  69.8 us
    unnamed x13, waiting for transfers between devices  58.7 us
  transfers between devices with their start and end apart: 11, of which 10 were waited for; matrix products, arithmetic and copies ran while one was open for 9% of the time, Pallas kernels for 0%

profile of v1, /device:TPU:0, one launch (start us, length us, event | category | flops | bytes accessed | tf_op | source)
XLA Modules:
  0.0 1927.4 jit_solution(1003487508710149438)
XLA Ops:
  11.8 3.3 fusion.130
  21.5 8.5 fusion.11
  30.0 14.4 fusion.3
  45.1 4.1 convert_bitcast_fusion.1
  55.6 31.1 %fusion.242 = (f32[12,512]{1,0:T(8,128)S(1)}, f32[12,512,512]{1,2,0:T(8,128)}) fusion(f32[512,512,12]{0,2,1:T(8,128)} %fusion.3, f32[512,512,12]{0,2,1:T(8,128)} %fusion.11, bf16[1,512,12,64]{3,1,2,0:T(8,128)(2,1)} %copy.153, bf16[1,512,12,64]{3,1,2,0:T(8,128)(2,1)} %copy.152, bf16[1,512,12,64]{3,1,2,0:T(8,128)(2,1)} %copy.150, ...), kind=kOutput, calls=%fused_computation.338 | convolution fusion | flops 827320320 | bytes 40919552 | tf_op jit(solution)/shard_map/while/body/eval_jaxpr/qhd,khd->hqk/dot_general | solution.py:23
  86.8 6.6 fusion.18
  100.4 3.1 fusion.127
  113.5 8.6 fusion.10
  122.1 14.4 fusion.2
  136.5 18.2 all-reduce.9.cloned.1.call-done
  157.6 20.2 %multiply_convert_fusion.3 = (bf16[512,3072]{1,0:T(8,128)(2,1)S(1)}, f32[512,3072]{1,0:T(8,128)}, f32[512,3072]{1,0:T(8,128)}) fusion(bf16[1,2,768,3072]{3,2,1,0:T(8,128)(2,1)} %param.22, f32[512,768]{1,0:T(8,128)S(1)} %get-tuple-element.221, f32[768]{0:T(1024)S(1)} %get-tuple-element.202, f32[768]{0:T(1024)S(1)} %get-tuple-element.267, ...), kind=kOutput, calls=%fused_computation.71 | convolution fusion | flops 2520121344 | bytes 22030336 | tf_op jit(solution)/shard_map/dot_general | solution.py:116
  181.7 4.1 convert_bitcast_fusion
  196.1 30.3 %fusion.244 = (f32[12,512]{1,0:T(8,128)S(1)}, f32[12,512,512]{1,2,0:T(8,128)}) fusion(f32[512,512,12]{0,2,1:T(8,128)} %fusion.2, f32[512,512,12]{0,2,1:T(8,128)} %fusion.10, bf16[1,512,12,64]{3,1,2,0:T(8,128)(2,1)S(1)} %copy-done.13, bf16[1,512,12,64]{3,1,2,0:T(8,128)(2,1)} %copy.169, bf16[1,512,12,64]{3,1,2,0:T(8,128)(2,1)S(1)} %copy-done.12, ...), kind=kOutput, calls=%fused_computation.340 | convolution fusion | flops 827320320 | bytes 40919552 | tf_op jit(solution)/shard_map/while/body/eval_jaxpr/qhd,khd->hqk/dot_general | solution.py:23
  226.5 6.6 fusion.19
  234.6 3.8 fusion.161
  241.4 51.6 %all-reduce.11.cloned.1.call-done = f32[512,768]{1,0:T(8,128)} async-done(((f32[512,768]{1,0:T(8,128)}), f32[512,768]{1,0:T(8,128)}) %all-reduce.11.cloned.1.call-update) | async-done | bytes 1572880 | tf_op jit(solution)/shard_map/psum | solution.py:112
  296.0 20.2 %multiply_convert_fusion.2 = (bf16[512,3072]{1,0:T(8,128)(2,1)S(1)}, f32[512,3072]{1,0:T(8,128)}, f32[512,3072]{1,0:T(8,128)}) fusion(bf16[1,2,768,3072]{3,2,1,0:T(8,128)(2,1)} %param.22, f32[512,768]{1,0:T(8,128)S(1)} %get-tuple-element.217, f32[768]{0:T(1024)S(1)} %get-tuple-element.203, f32[768]{0:T(1024)S(1)} %get-tuple-element.266, ...), kind=kOutput, calls=%fused_computation.58 | convolution fusion | flops 2520121344 | bytes 22030336 | tf_op jit(solution)/shard_map/dot_general | solution.py:116
  322.4 8.8 add_convert_fusion.1
  331.2 7.2 multiply_reduce_fusion.2
  340.6 51.5 %all-reduce.13.cloned.1.call-done = f32[512,768]{1,0:T(8,128)} async-done(((f32[512,768]{1,0:T(8,128)}), f32[512,768]{1,0:T(8,128)}) %all-reduce.13.cloned.1.call-update) | async-done | bytes 1572880 | tf_op jit(solution)/shard_map/psum | solution.py:170
  392.2 3.5 convolution_convert_fusion.1
  397.9 12.2 multiply_reduce_fusion.1
  410.2 7.3 multiply_convert_fusion.1
  417.5 3.1 fusion.135
  420.7 3.5 fusion.136
  424.2 3.0 fusion.155
  436.8 5.2 multiply_reduce_fusion.3
  442.8 10.2 add_convert_fusion
  453.1 5.1 multiply_reduce_fusion.4
  464.9 5.5 convolution_bitcast_fusion.6
  470.4 4.5 fusion.86
  474.9 5.1 convolution_bitcast_fusion.4
  480.0 10.0 maximum_bitcast_fusion.1
  490.0 21.8 %all-reduce.15.cloned.1.call-done = f32[512,768]{1,0:T(8,128)} async-done(((f32[512,768]{1,0:T(8,128)}), f32[512,768]{1,0:T(8,128)}) %all-reduce.15.cloned.1.call-update) | async-done | bytes 1572880 | tf_op jit(solution)/shard_map/psum | solution.py:170
  511.8 3.5 convolution_convert_fusion
  516.7 10.8 multiply_reduce_fusion
  529.8 7.2 multiply_convert_fusion
  541.3 3.5 fusion.138
  544.8 4.2 fusion.158
  556.8 5.1 convolution_bitcast_fusion.7
  562.0 3.1 fusion.121
  576.8 7.3 convolution_bitcast_fusion.5
  584.0 10.0 maximum_bitcast_fusion
  594.0 16.5 pad_maximum_fusion
  610.5 35.0 %copy.204 = f32[2,5,768,768]{3,0,1,2:T(2,128)} copy(f32[2,5,768,768]{2,3,1,0:T(8,128)} %pad_maximum_fusion) | data formatting | bytes 47185920 | tf_op jit(solution)/shard_map/stack | solution.py:281
  645.5 6.0 pad_maximum_fusion.3
  655.9 3.3 convolution_bitcast_fusion.8
  662.7 500.4 %all-reduce.19.cloned.1.call-done = (f32[2,1024,768]{2,1,0:T(8,128)}, f32[2,5,768,768]{3,0,1,2:T(2,128)}) async-done(((f32[2,1024,768]{2,1,0:T(8,128)}, f32[2,5,768,768]{3,0,1,2:T(2,128)}), (f32[2,1024,768]{2,1,0:T(8,128)}, f32[2,5,768,768]{3,0,1,2:T(2,128)})) %all-reduce.19.cloned.1.call-update) | async-done | bytes 29884432 | tf_op jit(solution)/shard_map/psum | solution.py:296
  1163.8 5.2 convolution_bitcast_fusion
  1171.8 6.7 pad_maximum_fusion.2
  1179.2 5.4 convolution_bitcast_fusion.2
  1187.5 7.2 pad_maximum_fusion.1
  1196.6 10.1 fusion.177
  1206.8 14.1 fusion.183
  1223.8 57.2 %reduce-scatter.16.cloned.1.call-done = f32[48,4]{1,0:T(8,128)} async-done(((f32[768,4]{1,0:T(8,128)}), f32[48,4]{1,0:T(8,128)}) %reduce-scatter.16.cloned.1.call-update) | async-done | bytes 784
  1282.4 10.0 fusion.174
  1292.5 14.2 fusion.180
  1306.8 58.5 %psum.62 = f32[2,2,12,96]{3,1,2,0:T(2,128)S(1)} all-reduce(f32[2,2,12,96]{3,1,2,0:T(2,128)S(1)} %broadcast_multiply_fusion), channel_id=1, replica_groups=mesh['stream'=2,'dp'=16] {'dp'}, use_global_device_ids=true, to_apply=%region_42.43 | all-reduce | flops 4608 | bytes 36864 | tf_op jit(solution)/shard_map/psum | solution.py:296
  1365.4 8.7 psum.63
  1374.6 5.9 fusion.122
  1383.7 132.1 %all-reduce.17.cloned.1.call-done = f32[2,1024,768]{2,1,0:T(8,128)} async-done(((f32[2,1024,768]{2,1,0:T(8,128)}), f32[2,1024,768]{2,1,0:T(8,128)}) %all-reduce.17.cloned.1.call-update) | async-done | bytes 6291472 | tf_op jit(solution)/shard_map/psum | solution.py:295
  1515.7 199.9 %reduce-scatter.14.cloned.1.call-done = f32[2,192,768]{2,1,0:T(8,128)} async-done(((f32[2,3072,768]{2,1,0:T(8,128)}), f32[2,192,768]{2,1,0:T(8,128)}) %reduce-scatter.14.cloned.1.call-update) | async-done | bytes 1179664 | tf_op jit(solution)/shard_map/reduce_scatter | solution.py:286
  1715.6 199.2 %reduce-scatter.12.cloned.1.call-done = f32[2,48,3072]{2,1,0:T(8,128)} async-done(((f32[2,768,3072]{2,1,0:T(8,128)}), f32[2,48,3072]{2,1,0:T(8,128)}) %reduce-scatter.12.cloned.1.call-update) | async-done | bytes 1179664 | tf_op jit(solution)/shard_map/reduce_scatter | solution.py:285
  1914.8 5.9 copy.281
  (384 shorter events, 137.9 us)
Async XLA Ops:
  7.2 147.5 %all-reduce.9.cloned.1.call-start = ((), (), s32[]{:S(2)}) async-start(), calls=%async_computation.5 | async-start | bytes 3145728 | tf_op jit(solution)/shard_map/psum | solution.py:112
  19.5 94.0 %copy-start.4 = (s32[512,512]{0,1:T(8,128)}, s32[512,512]{0,1:T(8,128)S(1)}, u32[]{:S(2)}) copy-start(s32[512,512]{0,1:T(8,128)S(1)} %copy.154) | copy-start | bytes 3145732
  21.4 100.7 %copy-start.6 = (s32[512,512]{0,1:T(8,128)}, s32[512,512]{0,1:T(8,128)S(1)}, u32[]{:S(2)}) copy-start(s32[512,512]{0,1:T(8,128)S(1)} %copy.157) | copy-start | bytes 3145732
  30.0 15.1 copy-start.44
  50.5 42.9 %copy-start.28 = (bf16[1,512,768]{1,2,0:T(8,128)(2,1)}, bf16[1,512,768]{1,2,0:T(8,128)(2,1)S(1)}, u32[]{:S(2)}) copy-start(bf16[1,512,768]{1,2,0:T(8,128)(2,1)S(1)} %get-tuple-element.227) | copy-start | bytes 2359300
  86.7 6.7 copy-start.54
  86.8 8.2 copy-start
  100.3 192.7 %all-reduce.11.cloned.1.call-start = ((), (), s32[]{:S(2)}) async-start(), calls=%async_computation.6 | async-start | bytes 3145728 | tf_op jit(solution)/shard_map/psum | solution.py:112
  106.7 6.1 copy-start.76
  113.5 64.3 %copy-start.70 = (f32[768]{0:T(1024)}, f32[768]{0:T(1024)S(1)}, u32[]{:S(2)}) copy-start(f32[768]{0:T(1024)S(1)} %get-tuple-element.267) | copy-start | bytes 9220
  113.5 64.3 %copy-start.81 = (f32[768]{0:T(1024)}, f32[768]{0:T(1024)S(1)}, u32[]{:S(2)}) copy-start(f32[768]{0:T(1024)S(1)} %get-tuple-element.202) | copy-start | bytes 9220
  113.5 202.6 %copy-start.83 = (f32[768]{0:T(1024)}, f32[768]{0:T(1024)S(1)}, u32[]{:S(2)}) copy-start(f32[768]{0:T(1024)S(1)} %get-tuple-element.203) | copy-start | bytes 9220
  113.5 224.9 %copy-start.72 = (f32[768]{0:T(1024)}, f32[768]{0:T(1024)S(1)}, u32[]{:S(2)}) copy-start(f32[768]{0:T(1024)S(1)} %get-tuple-element.266) | copy-start | bytes 9220
  122.1 32.6 %copy-start.45 = (bf16[1,1,512,768]{3,2,1,0:T(8,128)(2,1)S(1)}, bf16[1,1,512,768]{3,2,1,0:T(8,128)(2,1)}, u32[]{:S(2)}) copy-start(bf16[1,1,512,768]{3,2,1,0:T(8,128)(2,1)} %param.14) | copy-start | bytes 2359300
  154.7 23.1 %slice-start.6 = ((s8[9437184]{0:T(1024)(128)(4,1)}), s8[4194304]{0:T(1024)(128)(4,1)S(1)}, s32[]{:S(2)}) async-start(s8[9437184]{0:T(1024)(128)(4,1)} %bitcast.390), calls=%async_computation.22 | async-start | bytes 8388608
  156.5 21.3 %copy-start.16 = (f32[512,768]{1,0:T(8,128)}, f32[512,768]{1,0:T(8,128)S(1)}, u32[]{:S(2)}) copy-start(f32[512,768]{1,0:T(8,128)S(1)} %get-tuple-element.221) | copy-start | bytes 4718596
  156.5 21.3 %copy-start.60 = (f32[512]{0:T(512)}, f32[512]{0:T(512)S(1)}, u32[]{:S(2)}) copy-start(f32[512]{0:T(512)S(1)} %broadcast_multiply_fusion.4) | copy-start | bytes 6148
  157.6 20.2 %copy-start.77 = (f32[512]{0:T(512)}, f32[512]{0:T(512)S(1)}, u32[]{:S(2)}) copy-start(f32[512]{0:T(512)S(1)} %fusion.198) | copy-start | bytes 6148
  157.6 20.3 %slice-start.7 = ((s8[9437184]{0:T(1024)(128)(4,1)}), s8[4194304]{0:T(1024)(128)(4,1)S(1)}, s32[]{:S(2)}) async-start(s8[9437184]{0:T(1024)(128)(4,1)} %bitcast.390), calls=%async_computation.23 | async-start | bytes 8388608
  157.6 20.3 %slice-start.8 = ((s8[9437184]{0:T(1024)(128)(4,1)}), s8[1048576]{0:T(1024)(128)(4,1)S(1)}, s32[]{:S(2)}) async-start(s8[9437184]{0:T(1024)(128)(4,1)} %bitcast.390), calls=%async_computation.24 | async-start | bytes 2097152
  188.9 7.2 copy-start.12
  188.9 7.2 copy-start.13
  226.5 8.2 copy-start.1
  241.4 150.8 %all-reduce.13.cloned.1.call-start = ((), (), s32[]{:S(2)}) async-start(), calls=%async_computation.7 | async-start | bytes 3145728 | tf_op jit(solution)/shard_map/psum | solution.py:170
  293.0 23.1 %slice-start.9 = ((s8[9437184]{0:T(1024)(128)(4,1)}), s8[4194304]{0:T(1024)(128)(4,1)S(1)}, s32[]{:S(2)}) async-start(s8[9437184]{0:T(1024)(128)(4,1)} %bitcast.392), calls=%async_computation.25 | async-start | bytes 8388608
  295.6 42.8 %copy-start.18 = (f32[512,768]{1,0:T(8,128)}, f32[512,768]{1,0:T(8,128)S(1)}, u32[]{:S(2)}) copy-start(f32[512,768]{1,0:T(8,128)S(1)} %get-tuple-element.217) | copy-start | bytes 4718596
  295.6 42.8 %copy-start.62 = (f32[512]{0:T(512)}, f32[512]{0:T(512)S(1)}, u32[]{:S(2)}) copy-start(f32[512]{0:T(512)S(1)} %broadcast_multiply_fusion.2) | copy-start | bytes 6148
  295.9 42.5 %copy-start.79 = (f32[512]{0:T(512)}, f32[512]{0:T(512)S(1)}, u32[]{:S(2)}) copy-start(f32[512]{0:T(512)S(1)} %fusion.200) | copy-start | bytes 6148
  295.9 20.2 %slice-start.10 = ((s8[9437184]{0:T(1024)(128)(4,1)}), s8[4194304]{0:T(1024)(128)(4,1)S(1)}, s32[]{:S(2)}) async-start(s8[9437184]{0:T(1024)(128)(4,1)} %bitcast.392), calls=%async_computation.26 | async-start | bytes 8388608
  295.9 20.2 %slice-start.11 = ((s8[9437184]{0:T(1024)(128)(4,1)}), s8[1048576]{0:T(1024)(128)(4,1)S(1)}, s32[]{:S(2)}) async-start(s8[9437184]{0:T(1024)(128)(4,1)} %bitcast.392), calls=%async_computation.27 | async-start | bytes 2097152
  322.4 8.8 copy-start.39
  322.4 8.8 copy-start.87
  331.2 7.2 copy-start.97
  340.5 171.3 %all-reduce.15.cloned.1.call-start = ((), (), s32[]{:S(2)}) async-start(), calls=%async_computation.8 | async-start | bytes 3145728 | tf_op jit(solution)/shard_map/psum | solution.py:170
  397.9 12.2 slice-start.3
  397.9 12.2 slice-start.4
  397.9 12.2 slice-start.5
  410.2 7.3 copy-start.15
  429.4 7.4 copy-start.20
  429.4 7.4 copy-start.24
  436.8 16.2 slice-start.12
  436.8 16.2 slice-start.13
  442.7 10.3 copy-start.40
  442.7 10.3 copy-start.17
  442.7 10.3 copy-start.61
  442.8 10.3 copy-start.71
  442.8 10.3 copy-start.78
  442.8 10.3 slice-start.14
  460.2 703.0 %all-reduce.19.cloned.1.call-start = ((), (), s32[]{:S(2)}) async-start(), calls=%async_computation.15 | async-start | bytes 59768832 | tf_op jit(solution)/shard_map/psum | solution.py:296
  516.7 10.8 copy-start.23
  516.7 10.8 slice-start
  516.7 11.9 slice-start.1
  516.7 13.1 slice-start.2
  529.8 7.2 copy-start.9
  529.8 7.2 copy-start.11
  651.5 570.8 %reduce-scatter.18.cloned.1.call-start = ((), (), s32[]{:S(2)}) async-start(), calls=%async_computation.14 | async-start | bytes 417792
  654.0 626.9 %reduce-scatter.16.cloned.1.call-start = ((), (), s32[]{:S(2)}) async-start(), calls=%async_computation.13 | async-start | bytes 417792
  655.8 727.9 %reduce-scatter.10.cloned.1.call-start = ((), (), s32[]{:S(2)}) async-start(), calls=%async_computation.10 | async-start | bytes 5013504 | tf_op jit(solution)/shard_map/reduce_scatter | solution.py:284
  662.7 853.1 %all-reduce.17.cloned.1.call-start = ((), (), s32[]{:S(2)}) async-start(), calls=%async_computation.9 | async-start | bytes 12582912 | tf_op jit(solution)/shard_map/psum | solution.py:295
  1163.2 552.5 %reduce-scatter.14.cloned.1.call-start = ((), (), s32[]{:S(2)}) async-start(), calls=%async_computation.12 | async-start | bytes 20054016 | tf_op jit(solution)/shard_map/reduce_scatter | solution.py:286
  1178.5 736.3 %reduce-scatter.12.cloned.1.call-start = ((), (), s32[]{:S(2)}) async-start(), calls=%async_computation.11 | async-start | bytes 20054016 | tf_op jit(solution)/shard_map/reduce_scatter | solution.py:285
  1196.6 10.2 copy-start.7
  1292.5 82.2 %copy-start.46 = (bf16[1,512,768]{2,1,0:T(8,128)(2,1)S(1)}, bf16[1,512,768]{2,1,0:T(8,128)(2,1)}, u32[]{:S(2)}) copy-start(bf16[1,512,768]{2,1,0:T(8,128)(2,1)} %copy.192) | copy-start | bytes 2359300
  1292.5 82.2 %copy-start.47 = (bf16[1,512,768]{2,1,0:T(8,128)(2,1)S(1)}, bf16[1,512,768]{2,1,0:T(8,128)(2,1)}, u32[]{:S(2)}) copy-start(bf16[1,512,768]{2,1,0:T(8,128)(2,1)} %copy.193) | copy-start | bytes 2359300
  (65 other events, 209.5 us)
Sparse Core Ops, SparseCore 0:
  100.5 54.1 all-reduce.8
  241.5 51.4 all-reduce.10
  340.6 51.4 all-reduce.12
  460.3 51.4 all-reduce.14
  651.6 511.4 all-reduce.18
  1166.9 55.3 reduce-scatter.17
  1226.3 54.5 reduce-scatter.15
  1285.8 75.1 reduce-scatter.9
  1363.5 152.2 all-reduce.16
  1520.8 194.7 reduce-scatter.13
  1720.9 193.8 reduce-scatter.11
